TPU v7x, 32 devices: a whole 2x2x4 slice. The times are simulated.
32 devices in a mesh: dp: 16 (over z, y, x), mp: 2 (over core).
Axes of the slice: x: 2, y: 2, z: 4, core: 2. Of those that a mesh axis runs over, the one named last changes fastest.
Arguments:
- tokens: bfloat16 [36864, 768], P(('dp', 'mp')), may hold values from -6 to 6
- lengths: int32 [64], P('dp'), may hold values from 256 to 576, as said below
- gain_attn: float32 [768], replicated, may hold values from 0.5 to 1.5
- w_query: bfloat16 [768, 768], P(None, 'mp'), may hold values from -0.21875 to 0.21875
- w_key: bfloat16 [768, 768], P(None, 'mp'), may hold values from -0.21875 to 0.21875
- w_value: bfloat16 [768, 768], P(None, 'mp'), may hold values from -0.21875 to 0.21875
- w_out: bfloat16 [768, 768], P('mp'), may hold values from -1.75 to 1.75
- gain_ffn: float32 [768], replicated, may hold values from 0.5 to 1.5
- w_gate: bfloat16 [768, 2048], P(None, 'mp'), may hold values from -0.21875 to 0.21875
- w_up: bfloat16 [768, 2048], P(None, 'mp'), may hold values from -0.21875 to 0.21875
- w_down: bfloat16 [2048, 768], P('mp'), may hold values from -0.125 to 0.125
- cotangent: bfloat16 [36864, 768], P(('dp', 'mp')), may hold values from -6 to 6
Outputs:
- output: bfloat16 [36864, 768], P(('dp', 'mp'))
- grad_input: float32 [36864, 768], P(('dp', 'mp'))
- grad_gain_attn: float32 [768], replicated
- grad_query: float32 [768, 768], P('dp', 'mp')
- grad_key: float32 [768, 768], P('dp', 'mp')
- grad_value: float32 [768, 768], P('dp', 'mp')
- grad_out: float32 [768, 768], P('mp', 'dp')
- grad_gain_ffn: float32 [768], replicated
- grad_gate: float32 [768, 2048], P('dp', 'mp')
- grad_up: float32 [768, 2048], P('dp', 'mp')
- grad_down: float32 [2048, 768], P('mp', 'dp')
Inputs may be any that keep to these rules, and one draw needn't show every extreme that they name: `lengths`: each item's count of valid tokens, the class token first; exactly half of the 64 items have 576 and the other half 256.
All inputs are finite; a program needn't handle non-finite values.
Results may differ from a plain program's by a relative error of at most 0.013.
Values may be sent and summed in bfloat16 or wider, within the bound.
No kernel may reach another device: no remote copies, remote signals or barrier semaphores. Data moves between devices by JAX's collectives and lax.ppermute only.
A program may use at most 192 MiB of HBM per device.

v0:
```python
import jax
import jax.numpy as jnp
from jax import lax
from jax.sharding import PartitionSpec as P

HEAD = 64
SLOTS = 576
EPS = 1e-05
THETA = 10000.0


def tables(row_count):
    places = (jnp.arange(row_count) % SLOTS).astype(jnp.float32)
    inv_freq = THETA ** (-(2.0 * jnp.arange(HEAD // 2).astype(jnp.float32)) / HEAD)
    angles = places[:, None] * inv_freq[None, :]
    return (jnp.cos(angles), jnp.sin(angles))


def rotate(values, cosine, sine):
    half_width = values.shape[-1] // 2
    first_half = values[..., :half_width]
    second = values[..., half_width:]
    cos_b = cosine[:, None, :]
    sin_b = sine[:, None, :]
    return jnp.concatenate(
        [first_half * cos_b - second * sin_b, second * cos_b + first_half * sin_b], -1
    )


def unrotate(values, cosine, sine):
    half_width = values.shape[-1] // 2
    first_half = values[..., :half_width]
    second = values[..., half_width:]
    cos_b = cosine[:, None, :]
    sin_b = sine[:, None, :]
    return jnp.concatenate(
        [first_half * cos_b + second * sin_b, second * cos_b - first_half * sin_b], -1
    )


def contract_rows(left, right):
    return lax.dot_general(
        left, right, (((0,), (0,)), ((), ())), preferred_element_type=jnp.float32
    )


def contract_cols(left, right):
    return lax.dot_general(
        left, right, (((1,), (1,)), ((), ())), preferred_element_type=jnp.float32
    )


def norm_back(inputs, inv_rms, gain, d_normed):
    weighted = d_normed * gain
    d_inputs = inv_rms * weighted - inputs * inv_rms**3 * jnp.mean(
        weighted * inputs, -1, keepdims=True
    )
    d_gain = jnp.sum(d_normed * inputs * inv_rms, 0)
    return (d_inputs, d_gain)


def local(
    tokens,
    lengths,
    gain_attn,
    w_query,
    w_key,
    w_value,
    w_out,
    gain_ffn,
    w_gate,
    w_up,
    w_down,
    cotangent,
):
    half_rows = tokens.shape[0]
    score_scale = HEAD ** (-0.5)
    q_weight, k_weight, v_weight, o_weight = (w_query, w_key, w_value, w_out)
    g_weight, u_weight, d_weight = (w_gate, w_up, w_down)
    local_cols = q_weight.shape[1]
    head_count = local_cols // HEAD
    resid_in = tokens.astype(jnp.float32)
    inv_rms_a = lax.rsqrt(jnp.mean(resid_in * resid_in, -1, keepdims=True) + EPS)
    normed_a = (resid_in * inv_rms_a * gain_attn).astype(jnp.bfloat16)
    gathered_a = lax.all_gather(normed_a, "mp", axis=0, tiled=True)
    all_rows = gathered_a.shape[0]
    item_count = all_rows // SLOTS
    item_shape = (item_count, SLOTS, head_count, HEAD)
    cosine, sine = tables(all_rows)
    queries = rotate(
        jnp.dot(gathered_a, q_weight, preferred_element_type=jnp.float32).reshape(
            all_rows, head_count, HEAD
        ),
        cosine,
        sine,
    ).astype(jnp.bfloat16)
    key_heads = rotate(
        jnp.dot(gathered_a, k_weight, preferred_element_type=jnp.float32).reshape(
            all_rows, head_count, HEAD
        ),
        cosine,
        sine,
    ).astype(jnp.bfloat16)
    value_heads = jnp.dot(gathered_a, v_weight, preferred_element_type=jnp.float32).astype(
        jnp.bfloat16
    )
    q_items = queries.reshape(item_shape)
    k_items = key_heads.reshape(item_shape)
    v_items = value_heads.reshape(item_shape)
    places = jnp.arange(SLOTS)

    def masked_scores(q_item, k_item, length):
        scores = (
            jnp.einsum("qhd,khd->hqk", q_item, k_item, preferred_element_type=jnp.float32)
            * score_scale
        )
        allowed = (places[None, :] <= places[:, None]) & (places[None, :] < length)
        return jnp.where(allowed[None], scores, -1e30)

    def attend(item_args):
        q_item, k_item, v_item, length = item_args
        scores = masked_scores(q_item, k_item, length)
        top_score = jnp.max(scores, -1, keepdims=True)
        expo = jnp.exp(scores - top_score)
        total = jnp.sum(expo, -1, keepdims=True)
        soft_probs = (expo / total).astype(jnp.bfloat16)
        mixed_item = jnp.einsum(
            "hqk,khd->qhd", soft_probs, v_item, preferred_element_type=jnp.float32
        )
        return (mixed_item.astype(jnp.bfloat16), (top_score + jnp.log(total))[..., 0])

    mixed_heads, log_norm = lax.map(attend, (q_items, k_items, v_items, lengths))
    attn_rows = mixed_heads.reshape(all_rows, local_cols)
    attn_branch = lax.psum_scatter(
        jnp.dot(attn_rows, o_weight, preferred_element_type=jnp.float32),
        "mp",
        scatter_dimension=0,
        tiled=True,
    )
    middle = resid_in + attn_branch
    inv_rms_f = lax.rsqrt(jnp.mean(middle * middle, -1, keepdims=True) + EPS)
    normed_f = (middle * inv_rms_f * gain_ffn).astype(jnp.bfloat16)
    gathered_f = lax.all_gather(normed_f, "mp", axis=0, tiled=True)
    gate_pre = jnp.dot(gathered_f, g_weight, preferred_element_type=jnp.float32)
    up_pre = jnp.dot(gathered_f, u_weight, preferred_element_type=jnp.float32)
    sigmoid_g = jax.nn.sigmoid(gate_pre)
    silu_g = gate_pre * sigmoid_g
    hidden = (silu_g * up_pre).astype(jnp.bfloat16)
    ffn_branch = lax.psum_scatter(
        jnp.dot(hidden, d_weight, preferred_element_type=jnp.float32).astype(jnp.bfloat16),
        "mp",
        scatter_dimension=0,
        tiled=True,
    ).astype(jnp.float32)
    row_index = lax.axis_index("mp") * half_rows + jnp.arange(half_rows)
    final_rows = middle + ffn_branch
    owner = (row_index // SLOTS)[:, None] == jnp.arange(item_count)[None, :]
    limit = jnp.sum(jnp.where(owner, lengths[None, :], 0), 1)
    valid_rows = (row_index % SLOTS < limit).astype(jnp.float32)[:, None]
    output = (valid_rows * final_rows).astype(jnp.bfloat16)
    d_final = valid_rows * cotangent.astype(jnp.float32)
    d_ffn_all = lax.all_gather(d_final.astype(jnp.bfloat16), "mp", axis=0, tiled=True)
    grad_down = contract_rows(hidden, d_ffn_all)
    d_hidden = contract_cols(d_ffn_all, d_weight)
    d_gate = (d_hidden * up_pre * (sigmoid_g * (1.0 + gate_pre * (1.0 - sigmoid_g)))).astype(
        jnp.bfloat16
    )
    d_up = (d_hidden * silu_g).astype(jnp.bfloat16)
    grad_gate = contract_rows(gathered_f, d_gate)
    grad_up = contract_rows(gathered_f, d_up)
    ffn_sums = (
        lax.psum_scatter(grad_gate, "dp", scatter_dimension=0, tiled=True),
        lax.psum_scatter(grad_up, "dp", scatter_dimension=0, tiled=True),
        lax.psum_scatter(grad_down, "dp", scatter_dimension=1, tiled=True),
    )
    d_normed_f = lax.psum_scatter(
        contract_cols(d_gate, g_weight) + contract_cols(d_up, u_weight),
        "mp",
        scatter_dimension=0,
        tiled=True,
    )
    d_middle_norm, d_gain_ffn = norm_back(middle, inv_rms_f, gain_ffn, d_normed_f)
    d_middle = d_final + d_middle_norm
    d_attn_all = lax.all_gather(d_middle.astype(jnp.bfloat16), "mp", axis=0, tiled=True)
    grad_out = contract_rows(attn_rows, d_attn_all)
    d_mixed = contract_cols(d_attn_all, o_weight).astype(jnp.bfloat16).reshape(item_shape)

    def attend_back(item_args):
        q_item, k_item, v_item, length, norm_item, d_item = item_args
        scores = masked_scores(q_item, k_item, length)
        soft_probs = jnp.exp(scores - norm_item[..., None])
        d_value = jnp.einsum(
            "hqk,qhd->khd",
            soft_probs.astype(jnp.bfloat16),
            d_item,
            preferred_element_type=jnp.float32,
        )
        d_soft = jnp.einsum("qhd,khd->hqk", d_item, v_item, preferred_element_type=jnp.float32)
        d_scores = (soft_probs * (d_soft - jnp.sum(soft_probs * d_soft, -1, keepdims=True))).astype(
            jnp.bfloat16
        )
        d_query = (
            jnp.einsum("hqk,khd->qhd", d_scores, k_item, preferred_element_type=jnp.float32)
            * score_scale
        )
        d_key = (
            jnp.einsum("hqk,qhd->khd", d_scores, q_item, preferred_element_type=jnp.float32)
            * score_scale
        )
        return (d_query, d_key, d_value)

    d_queries, d_keys, d_values = lax.map(
        attend_back, (q_items, k_items, v_items, lengths, log_norm, d_mixed)
    )
    d_q_rows = (
        unrotate(d_queries.reshape(all_rows, head_count, HEAD), cosine, sine)
        .astype(jnp.bfloat16)
        .reshape(all_rows, local_cols)
    )
    d_k_rows = (
        unrotate(d_keys.reshape(all_rows, head_count, HEAD), cosine, sine)
        .astype(jnp.bfloat16)
        .reshape(all_rows, local_cols)
    )
    d_v_rows = d_values.astype(jnp.bfloat16).reshape(all_rows, local_cols)
    grad_query = contract_rows(gathered_a, d_q_rows)
    grad_key = contract_rows(gathered_a, d_k_rows)
    grad_value = contract_rows(gathered_a, d_v_rows)
    d_normed_a = lax.psum_scatter(
        contract_cols(d_q_rows, q_weight)
        + contract_cols(d_k_rows, k_weight)
        + contract_cols(d_v_rows, v_weight),
        "mp",
        scatter_dimension=0,
        tiled=True,
    )
    d_input_norm, d_gain_attn = norm_back(resid_in, inv_rms_a, gain_attn, d_normed_a)
    grad_input = d_middle + d_input_norm
    gain_grads = lax.psum((d_gain_attn, d_gain_ffn), ("dp", "mp"))
    attn_sums = (
        lax.psum_scatter(grad_query, "dp", scatter_dimension=0, tiled=True),
        lax.psum_scatter(grad_key, "dp", scatter_dimension=0, tiled=True),
        lax.psum_scatter(grad_value, "dp", scatter_dimension=0, tiled=True),
        lax.psum_scatter(grad_out, "dp", scatter_dimension=1, tiled=True),
    )
    summed = (
        attn_sums[0],
        attn_sums[1],
        attn_sums[2],
        attn_sums[3],
        ffn_sums[0],
        ffn_sums[1],
        ffn_sums[2],
    )
    return (
        output,
        grad_input,
        gain_grads[0],
        summed[0],
        summed[1],
        summed[2],
        summed[3],
        gain_grads[1],
        summed[4],
        summed[5],
        summed[6],
    )


def solution(mesh):
    in_specs = (
        P(("dp", "mp"), None),
        P("dp"),
        P(),
        P(None, "mp"),
        P(None, "mp"),
        P(None, "mp"),
        P("mp", None),
        P(),
        P(None, "mp"),
        P(None, "mp"),
        P("mp", None),
        P(("dp", "mp"), None),
    )
    out_specs = (
        P(("dp", "mp"), None),
        P(("dp", "mp"), None),
        P(),
        P("dp", "mp"),
        P("dp", "mp"),
        P("dp", "mp"),
        P("mp", "dp"),
        P(),
        P("dp", "mp"),
        P("dp", "mp"),
        P("mp", "dp"),
    )
    return jax.shard_map(local, mesh=mesh, in_specs=in_specs, out_specs=out_specs, check_vma=False)
```

profile of v0, /device:TPU:0, one launch (start us, length us, event | category | flops | bytes accessed | tf_op | source)
XLA Modules:
  0.0 1483.8 jit_solution(9570107461674244627)
XLA Ops:
  10.4 3.2 fusion.61
  15.7 13.5 all-gather.5.cloned.1.call-done
  29.2 4.1 convolution_convert_fusion.2
  35.6 4.3 reshape.306
  41.6 3.8 fusion.82
  63.9 42.3 %while.30 = (s32[]{:T(128)}, bf16[4,576,6,64]{1,3,2,0:T(8,128)(2,1)S(1)}, f32[4,6,576]{2,1,0:T(8,128)}, bf16[4,576,6,64]{1,3,2,0:T(8,128)(2,1)}, s32[4]{0:T(128)...) while((s32[]{:T(128)}, ...), condition=%wide.region_5.6_spmd.clone.clone, body=%wide.region_2.5_spmd.clone.clone.sunk | while | flops 534377664 | bytes 28236528 | solution.py:132
  70.1 3.7 fusion.162
  80.6 3.7 fusion.162
  91.2 3.7 fusion.162
  101.8 3.7 fusion.162
  108.9 3.5 reshape.309
  112.5 6.4 fusion.83
  119.0 16.7 %reduce-scatter.12.cloned.1.call-done = f32[1152,768]{1,0:T(8,128)} async-done(((f32[2304,768]{1,0:T(8,128)}), f32[1152,768]{1,0:T(8,128)}) %reduce-scatter.12.cloned.1.call-update) | async-done | bytes 3538960 | tf_op jit(solution)/shard_map/reduce_scatter | solution.py:134
  143.7 11.9 all-gather.7.cloned.1.call-done
  155.6 10.5 fusion.85
  166.2 6.2 fusion.84
  172.4 14.8 multiply_convert_fusion.1
  187.2 7.5 fusion.86
  194.7 6.1 convolution_add_fusion
  201.1 7.7 convolution_convert_fusion
  208.8 8.7 reduce-scatter.16.cloned.1.call-done
  217.5 3.4 multiply_reduce_fusion.1
  221.6 10.8 reduce-scatter.14.cloned.1.call-done
  232.3 5.9 fusion.80
  238.3 13.9 all-gather.11.cloned.1.call-done
  252.3 4.2 convolution_convert_fusion.1
  258.8 4.3 reshape.310
  264.7 246.6 %while.31 = (s32[]{:T(128)}, f32[4,576,6,64]{1,0,3,2:T(4,128)}, f32[4,576,6,64]{1,0,3,2:T(4,128)}, bf16[4,576,6,64]{1,3,2,0:T(8,128)(2,1)}, bf16[4,576,6,64]{1,3...) while((s32[]{:T(128)}, f32[4,576,6,64]{1,0,3,2:T(4,128)}, ...), condition=%wide.region_13.14_spmd.clone.clone, body=%wide.region_11.13_spmd.clone.clone.sunk | while | flops 1304982784 | bytes 89503072 | solution.py:212
  270.0 3.5 fusion.175
  273.5 5.0 multiply_reduce_fusion.5
  287.4 19.6 %dynamic_update_slice.40 = f32[4,576,6,64]{1,0,3,2:T(4,128)} dynamic-update-slice(f32[4,576,6,64]{1,0,3,2:T(4,128)} %get-tuple-element.481, f32[1,576,6,64]{1,0,3,2:T(1,128)S(1)} %copy.81, s32[]{:T(128)S(6)} %copy.100, s32[]{:T(128)} %constant.88.clone.1..sunk, s32[]{:T(128)} %constant.88.clone.1..sunk, s32[]{:T(128)} %constant.88.clone.1..sunk) | dynamic-update-slice | bytes 1769476 | tf_op jit(solution)/shard_map/while/body/jit(dynamic_update_index_in_dim)/dynamic_update_slice | solution.py:212
  307.1 19.6 %dynamic_update_slice.39 = f32[4,576,6,64]{1,0,3,2:T(4,128)} dynamic-update-slice(f32[4,576,6,64]{1,0,3,2:T(4,128)} %get-tuple-element.480, f32[1,576,6,64]{1,0,3,2:T(1,128)S(1)} %copy.80, s32[]{:T(128)S(6)} %copy.100, s32[]{:T(128)} %constant.88.clone.1..sunk, s32[]{:T(128)} %constant.88.clone.1..sunk, s32[]{:T(128)} %constant.88.clone.1..sunk) | dynamic-update-slice | bytes 1769476 | tf_op jit(solution)/shard_map/while/body/jit(dynamic_update_index_in_dim)/dynamic_update_slice | solution.py:212
  331.5 3.5 fusion.175
  335.0 4.9 multiply_reduce_fusion.5
  348.9 19.6 %dynamic_update_slice.40 = f32[4,576,6,64]{1,0,3,2:T(4,128)} dynamic-update-slice(f32[4,576,6,64]{1,0,3,2:T(4,128)} %get-tuple-element.481, f32[1,576,6,64]{1,0,3,2:T(1,128)S(1)} %copy.81, s32[]{:T(128)S(6)} %copy.100, s32[]{:T(128)} %constant.88.clone.1..sunk, s32[]{:T(128)} %constant.88.clone.1..sunk, s32[]{:T(128)} %constant.88.clone.1..sunk) | dynamic-update-slice | bytes 1769476 | tf_op jit(solution)/shard_map/while/body/jit(dynamic_update_index_in_dim)/dynamic_update_slice | solution.py:212
  368.6 19.6 %dynamic_update_slice.39 = f32[4,576,6,64]{1,0,3,2:T(4,128)} dynamic-update-slice(f32[4,576,6,64]{1,0,3,2:T(4,128)} %get-tuple-element.480, f32[1,576,6,64]{1,0,3,2:T(1,128)S(1)} %copy.80, s32[]{:T(128)S(6)} %copy.100, s32[]{:T(128)} %constant.88.clone.1..sunk, s32[]{:T(128)} %constant.88.clone.1..sunk, s32[]{:T(128)} %constant.88.clone.1..sunk) | dynamic-update-slice | bytes 1769476 | tf_op jit(solution)/shard_map/while/body/jit(dynamic_update_index_in_dim)/dynamic_update_slice | solution.py:212
  393.0 3.5 fusion.175
  396.5 4.9 multiply_reduce_fusion.5
  410.4 19.6 %dynamic_update_slice.40 = f32[4,576,6,64]{1,0,3,2:T(4,128)} dynamic-update-slice(f32[4,576,6,64]{1,0,3,2:T(4,128)} %get-tuple-element.481, f32[1,576,6,64]{1,0,3,2:T(1,128)S(1)} %copy.81, s32[]{:T(128)S(6)} %copy.100, s32[]{:T(128)} %constant.88.clone.1..sunk, s32[]{:T(128)} %constant.88.clone.1..sunk, s32[]{:T(128)} %constant.88.clone.1..sunk) | dynamic-update-slice | bytes 1769476 | tf_op jit(solution)/shard_map/while/body/jit(dynamic_update_index_in_dim)/dynamic_update_slice | solution.py:212
  430.1 19.6 %dynamic_update_slice.39 = f32[4,576,6,64]{1,0,3,2:T(4,128)} dynamic-update-slice(f32[4,576,6,64]{1,0,3,2:T(4,128)} %get-tuple-element.480, f32[1,576,6,64]{1,0,3,2:T(1,128)S(1)} %copy.80, s32[]{:T(128)S(6)} %copy.100, s32[]{:T(128)} %constant.88.clone.1..sunk, s32[]{:T(128)} %constant.88.clone.1..sunk, s32[]{:T(128)} %constant.88.clone.1..sunk) | dynamic-update-slice | bytes 1769476 | tf_op jit(solution)/shard_map/while/body/jit(dynamic_update_index_in_dim)/dynamic_update_slice | solution.py:212
  454.5 3.5 fusion.175
  458.0 4.9 multiply_reduce_fusion.5
  471.9 19.6 %dynamic_update_slice.40 = f32[4,576,6,64]{1,0,3,2:T(4,128)} dynamic-update-slice(f32[4,576,6,64]{1,0,3,2:T(4,128)} %get-tuple-element.481, f32[1,576,6,64]{1,0,3,2:T(1,128)S(1)} %copy.81, s32[]{:T(128)S(6)} %copy.100, s32[]{:T(128)} %constant.88.clone.1..sunk, s32[]{:T(128)} %constant.88.clone.1..sunk, s32[]{:T(128)} %constant.88.clone.1..sunk) | dynamic-update-slice | bytes 1769476 | tf_op jit(solution)/shard_map/while/body/jit(dynamic_update_index_in_dim)/dynamic_update_slice | solution.py:212
  491.6 19.6 %dynamic_update_slice.39 = f32[4,576,6,64]{1,0,3,2:T(4,128)} dynamic-update-slice(f32[4,576,6,64]{1,0,3,2:T(4,128)} %get-tuple-element.480, f32[1,576,6,64]{1,0,3,2:T(1,128)S(1)} %copy.80, s32[]{:T(128)S(6)} %copy.100, s32[]{:T(128)} %constant.88.clone.1..sunk, s32[]{:T(128)} %constant.88.clone.1..sunk, s32[]{:T(128)} %constant.88.clone.1..sunk) | dynamic-update-slice | bytes 1769476 | tf_op jit(solution)/shard_map/while/body/jit(dynamic_update_index_in_dim)/dynamic_update_slice | solution.py:212
  517.1 4.1 reshape.311
  521.2 5.5 reshape.312
  534.9 5.1 add_add_fusion
  540.3 9.0 fusion.95
  549.4 10.8 fusion.93
  560.3 9.1 fusion.94
  569.7 5.2 fusion.92
  574.9 5.6 fusion.91
  580.6 5.1 fusion.89
  585.8 5.8 fusion.90
  591.7 3.4 fusion.67
  595.1 40.7 %all-reduce = (f32[768]{0:T(1024)}, f32[768]{0:T(1024)}) all-reduce(f32[768]{0:T(1024)S(1)} %get-tuple-element.261, f32[768]{0:T(1024)S(1)} %copy-done.27), channel_id=1, replica_groups=mesh['dp'=16,'mp'=2] {'dp','mp'}, use_global_device_ids=true, to_apply=%region_17.18 | all-reduce | flops 1536 | bytes 12288 | tf_op jit(solution)/shard_map/psum | solution.py:239
  635.7 5.0 fusion.64
  640.7 53.7 %reduce-scatter.32.cloned.1.call-done = f32[1024,48]{0,1:T(8,128)} async-done(((f32[1024,768]{0,1:T(8,128)}), f32[1024,48]{0,1:T(8,128)}) %reduce-scatter.32.cloned.1.call-update) | async-done | bytes 196624 | tf_op jit(solution)/shard_map/reduce_scatter | solution.py:174
  694.4 135.5 %reduce-scatter.28.cloned.1.call-done = f32[48,1024]{1,0:T(8,128)} async-done(((f32[768,1024]{1,0:T(8,128)}), f32[48,1024]{1,0:T(8,128)}) %reduce-scatter.28.cloned.1.call-update) | async-done | bytes 196624 | tf_op jit(solution)/shard_map/reduce_scatter | solution.py:172
  829.8 135.5 %reduce-scatter.30.cloned.1.call-done = f32[48,1024]{1,0:T(8,128)} async-done(((f32[768,1024]{1,0:T(8,128)}), f32[48,1024]{1,0:T(8,128)}) %reduce-scatter.30.cloned.1.call-update) | async-done | bytes 196624 | tf_op jit(solution)/shard_map/reduce_scatter | solution.py:173
  965.4 128.0 %reduce-scatter.26.cloned.1.call-done = f32[384,48]{0,1:T(8,128)} async-done(((f32[384,768]{0,1:T(8,128)}), f32[384,48]{0,1:T(8,128)}) %reduce-scatter.26.cloned.1.call-update) | async-done | bytes 73744 | tf_op jit(solution)/shard_map/reduce_scatter | solution.py:244
  1093.4 128.0 %reduce-scatter.24.cloned.1.call-done = f32[48,384]{1,0:T(8,128)} async-done(((f32[768,384]{1,0:T(8,128)}), f32[48,384]{1,0:T(8,128)}) %reduce-scatter.24.cloned.1.call-update) | async-done | bytes 73744 | tf_op jit(solution)/shard_map/reduce_scatter | solution.py:243
  1221.4 127.7 %reduce-scatter.20.cloned.1.call-done = f32[48,384]{1,0:T(8,128)} async-done(((f32[768,384]{1,0:T(8,128)}), f32[48,384]{1,0:T(8,128)}) %reduce-scatter.20.cloned.1.call-update) | async-done | bytes 73744 | tf_op jit(solution)/shard_map/reduce_scatter | solution.py:241
  1349.1 127.7 %reduce-scatter.22.cloned.1.call-done = f32[48,384]{1,0:T(8,128)} async-done(((f32[768,384]{1,0:T(8,128)}), f32[48,384]{1,0:T(8,128)}) %reduce-scatter.22.cloned.1.call-update) | async-done | bytes 73744 | tf_op jit(solution)/shard_map/reduce_scatter | solution.py:242
  (218 shorter events, 140.5 us)
Async XLA Ops:
  7.2 165.2 %copy-start = (bf16[1024,768]{1,0:T(8,128)(2,1)S(1)}, bf16[1024,768]{1,0:T(8,128)(2,1)}, u32[]{:S(2)}) copy-start(bf16[1024,768]{1,0:T(8,128)(2,1)} %param.26) | copy-start | bytes 4718596
  7.2 22.0 %all-gather.5.cloned.1.call-start = ((), (), s32[]{:S(2)}) async-start(), calls=%async_computation.11 | async-start | bytes 5308416 | tf_op jit(solution)/shard_map/all_gather | solution.py:85
  9.8 0.6 copy-start.22
  13.6 122.1 %reduce-scatter.12.cloned.1.call-start = ((), (), s32[]{:S(2)}) async-start(), calls=%async_computation.12 | async-start | bytes 10616832 | tf_op jit(solution)/shard_map/reduce_scatter | solution.py:134
  40.0 1.7 copy-start.19
  41.6 3.8 copy-start.17
  41.6 3.8 copy-start.30
  45.5 1.7 copy-start.12
  45.5 1.7 copy-start.13
  55.0 1.7 copy-start.11
  60.4 3.0 copy-start.28
  61.8 2.1 copy-start.14
  112.5 6.4 copy-start.6
  118.9 16.8 %copy-start.4 = (bf16[1152,768]{1,0:T(8,128)(2,1)S(1)}, bf16[1152,768]{1,0:T(8,128)(2,1)}, u32[]{:S(2)}) copy-start(bf16[1152,768]{1,0:T(8,128)(2,1)} %param.16) | copy-start | bytes 5308420
  118.9 21.1 %copy-start.24 = (f32[768]{0:T(1024)S(1)}, f32[768]{0:T(1024)}, u32[]{:S(2)}) copy-start(f32[768]{0:T(1024)} %param.23) | copy-start | bytes 9220
  118.9 36.7 %all-gather.7.cloned.1.call-start = ((), (), s32[]{:S(2)}) async-start(), calls=%async_computation.13 | async-start | bytes 5308416 | tf_op jit(solution)/shard_map/all_gather | solution.py:143
  138.2 1.8 copy-start.2
  140.0 1.9 copy-start.10
  141.6 30.8 %all-gather.9.cloned.1.call-start = ((), (), s32[]{:S(2)}) async-start(), calls=%async_computation.15 | async-start | bytes 5308416 | tf_op jit(solution)/shard_map/all_gather | solution.py:162
  143.5 22.7 %copy-start.32 = (bf16[768,1024]{1,0:T(8,128)(2,1)S(1)}, bf16[768,1024]{1,0:T(8,128)(2,1)}, u32[]{:S(2)}) copy-start(bf16[768,1024]{1,0:T(8,128)(2,1)} %param.24) | copy-start | bytes 4718596
  143.5 74.0 %reduce-scatter.16.cloned.1.call-start = ((), (), s32[]{:S(2)}) async-start(), calls=%async_computation.16 | async-start | bytes 10616832 | tf_op jit(solution)/shard_map/reduce_scatter | solution.py:176
  155.6 10.5 copy-start.31
  187.2 7.5 copy-start.34
  187.2 7.5 copy-start.33
  200.8 31.5 %reduce-scatter.14.cloned.1.call-start = ((), (), s32[]{:S(2)}) async-start(), calls=%async_computation.14 | async-start | bytes 5308416 | tf_op jit(solution)/shard_map/reduce_scatter | solution.py:149
  208.8 8.8 copy-start.3
  208.8 43.5 %all-gather.11.cloned.1.call-start = ((), (), s32[]{:S(2)}) async-start(), calls=%async_computation.17 | async-start | bytes 5308416 | tf_op jit(solution)/shard_map/all_gather | solution.py:184
  238.3 353.4 %reduce-scatter.18.cloned.1.call-start = ((), (), s32[]{:S(2)}) async-start(), calls=%async_computation.18 | async-start | bytes 10616832 | tf_op jit(solution)/shard_map/reduce_scatter | solution.py:229
  258.8 6.0 copy-start.29
  267.3 2.7 copy-start.15
  273.5 5.0 copy-start.16
  328.8 2.7 copy-start.15
  335.0 5.0 copy-start.16
  390.3 2.7 copy-start.15
  396.5 5.0 copy-start.16
  451.8 2.7 copy-start.15
  458.0 5.0 copy-start.16
  529.7 1.1 copy-start.18
  530.0 2.9 copy-start.8
  530.8 2.1 copy-start.20
  532.9 2.1 copy-start.9
  532.9 2.1 copy-start.21
  540.0 154.3 %reduce-scatter.32.cloned.1.call-start = ((), (), s32[]{:S(2)}) async-start(), calls=%async_computation.25 | async-start | bytes 3342336 | tf_op jit(solution)/shard_map/reduce_scatter | solution.py:174
  549.3 280.5 %reduce-scatter.28.cloned.1.call-start = ((), (), s32[]{:S(2)}) async-start(), calls=%async_computation.23 | async-start | bytes 3342336 | tf_op jit(solution)/shard_map/reduce_scatter | solution.py:172
  560.2 9.5 copy-start.7
  560.2 405.2 %reduce-scatter.30.cloned.1.call-start = ((), (), s32[]{:S(2)}) async-start(), calls=%async_computation.24 | async-start | bytes 3342336 | tf_op jit(solution)/shard_map/reduce_scatter | solution.py:173
  569.3 524.0 %reduce-scatter.26.cloned.1.call-start = ((), (), s32[]{:S(2)}) async-start(), calls=%async_computation.22 | async-start | bytes 1253376 | tf_op jit(solution)/shard_map/reduce_scatter | solution.py:244
  574.8 646.5 %reduce-scatter.24.cloned.1.call-start = ((), (), s32[]{:S(2)}) async-start(), calls=%async_computation.21 | async-start | bytes 1253376 | tf_op jit(solution)/shard_map/reduce_scatter | solution.py:243
  580.5 768.6 %reduce-scatter.20.cloned.1.call-start = ((), (), s32[]{:S(2)}) async-start(), calls=%async_computation.19 | async-start | bytes 1253376 | tf_op jit(solution)/shard_map/reduce_scatter | solution.py:241
  585.7 5.9 copy-start.5
  585.7 5.9 copy-start.23
  585.7 5.9 copy-start.25
  585.7 891.1 %reduce-scatter.22.cloned.1.call-start = ((), (), s32[]{:S(2)}) async-start(), calls=%async_computation.20 | async-start | bytes 1253376 | tf_op jit(solution)/shard_map/reduce_scatter | solution.py:242
  591.6 3.5 copy-start.27
  591.6 44.2 %copy-start.26 = (f32[1152]{0:T(1024)S(1)}, f32[1152]{0:T(1024)}, u32[]{:S(2)}) copy-start(f32[1152]{0:T(1024)} %get-tuple-element.325) | copy-start | bytes 13828
  635.7 841.1 %copy-start.1 = (bf16[1024,768]{1,0:T(8,128)(2,1)S(1)}, bf16[1024,768]{1,0:T(8,128)(2,1)}, u32[]{:S(2)}) copy-start(bf16[1024,768]{1,0:T(8,128)(2,1)} %param.26) | copy-start | bytes 4718596
Sparse Core Ops, SparseCore 0:
  13.7 15.3 all-gather.4
  119.0 16.6 reduce-scatter.11
  141.8 13.8 all-gather.6
  157.1 13.8 all-gather.8
  200.9 16.5 reduce-scatter.15
  219.6 12.6 reduce-scatter.13
  238.4 13.8 all-gather.10
  540.2 16.6 reduce-scatter.17
  562.4 131.9 reduce-scatter.31
  699.8 130.0 reduce-scatter.27
  835.4 129.9 reduce-scatter.29
  970.5 122.7 reduce-scatter.25
  1098.7 122.5 reduce-scatter.23
  1226.5 122.5 reduce-scatter.19
  1354.3 122.5 reduce-scatter.21
where the time goes:
time: 1500 us; the launch traced here: 1480 us
  waiting for transfers between devices  912 us (61%)
  local copies, waits for them, and re-layouts  225 us (15%)
  matrix products  221 us (15%)
  other arithmetic  67.5 us (4%)
  blocking collectives  40.7 us (3%)
    dynamic_update_slice x16, local copies, waits for them, and re-layouts, local(): lax.map(attend_back, (q_items, k_items, v_items, lengths, log_norm, d_mix...  165 us
    reduce_scatter x1, waiting for transfers between devices, local(): lax.psum_scatter(grad_up, 'dp', scatter_dimension=0, tiled=True)  136 us
    reduce_scatter x1, waiting for transfers between devices, local(): lax.psum_scatter(grad_gate, 'dp', scatter_dimension=0, tiled=True)  135 us
    reduce_scatter x1, waiting for transfers between devices, local(): lax.psum_scatter(grad_out, 'dp', scatter_dimension=1, tiled=True)  128 us
    reduce_scatter x1, waiting for transfers between devices, local(): lax.psum_scatter(grad_value, 'dp', scatter_dimension=0, tiled=True)  128 us
    reduce_scatter x1, waiting for transfers between devices, local(): lax.psum_scatter(grad_query, 'dp', scatter_dimension=0, tiled=True)  128 us
    reduce_scatter x1, waiting for transfers between devices, local(): lax.psum_scatter(grad_key, 'dp', scatter_dimension=0, tiled=True)  128 us
    reduce_scatter x1, waiting for transfers between devices, local(): lax.psum_scatter(grad_down, 'dp', scatter_dimension=1, tiled=True)  53.7 us
  transfers between devices with their start and end apart: 15, of which 13 were waited for; matrix products, arithmetic and copies ran while one was open for 6% of the time, Pallas kernels for 0%

commit v1 on v0

--- a/solution.py
+++ b/solution.py
@@ -236,7 +236,9 @@
     )
     d_input_norm, d_gain_attn = norm_back(resid_in, inv_rms_a, gain_attn, d_normed_a)
     grad_input = d_middle + d_input_norm
-    gain_grads = lax.psum((d_gain_attn, d_gain_ffn), ("dp", "mp"))
+    gain_grads = (d_gain_attn, d_gain_ffn)
+    for jj in ("dp", "mp"):
+        gain_grads = lax.psum(gain_grads, axis_name=jj)
     attn_sums = (
         lax.psum_scatter(grad_query, "dp", scatter_dimension=0, tiled=True),
         lax.psum_scatter(grad_key, "dp", scatter_dimension=0, tiled=True),

time: 1500 us -> 1500 us (level)
    psum x1 -> x2, blocking collectives: 40.7 us -> 46.1 us  [local(): gain_grads = lax.psum(gain_grads, axis_name=jj)]
where the time goes in v1:
time: 1500 us; the launch traced here: 1480 us
  waiting for transfers between devices  906 us (60%)
  local copies, waits for them, and re-layouts  225 us (15%)
  matrix products  221 us (15%)
  other arithmetic  67.5 us (4%)
  blocking collectives  46.1 us (3%)
    dynamic_update_slice x16, local copies, waits for them, and re-layouts, local(): lax.map(attend_back, (q_items, k_items, v_items, lengths, log_norm, d_mix...  165 us
    reduce_scatter x1, waiting for transfers between devices, local(): lax.psum_scatter(grad_up, 'dp', scatter_dimension=0, tiled=True)  136 us
    reduce_scatter x1, waiting for transfers between devices, local(): lax.psum_scatter(grad_gate, 'dp', scatter_dimension=0, tiled=True)  135 us
    reduce_scatter x1, waiting for transfers between devices, local(): lax.psum_scatter(grad_out, 'dp', scatter_dimension=1, tiled=True)  128 us
    reduce_scatter x1, waiting for transfers between devices, local(): lax.psum_scatter(grad_value, 'dp', scatter_dimension=0, tiled=True)  128 us
    reduce_scatter x1, waiting for transfers between devices, local(): lax.psum_scatter(grad_query, 'dp', scatter_dimension=0, tiled=True)  128 us
    reduce_scatter x1, waiting for transfers between devices, local(): lax.psum_scatter(grad_key, 'dp', scatter_dimension=0, tiled=True)  128 us
    dot_general x7, matrix products, contract_rows(): lax.dot_general(left, right, (((0,), (0,)), ((), ())), preferred_element_...  50.5 us
  transfers between devices with their start and end apart: 15, of which 13 were waited for; matrix products, arithmetic and copies ran while one was open for 6% of the time, Pallas kernels for 0%

profile of v1, /device:TPU:0, one launch (start us, length us, event | category | flops | bytes accessed | tf_op | source)
XLA Modules:
  0.0 1483.8 jit_solution(17902074403007894805)
XLA Ops:
  10.4 3.2 fusion.61
  15.6 13.5 all-gather.5.cloned.1.call-done
  29.2 4.1 convolution_convert_fusion.2
  35.6 4.3 reshape.306
  41.6 3.8 fusion.82
  63.8 42.3 %while.30 = (s32[]{:T(128)}, bf16[4,576,6,64]{1,3,2,0:T(8,128)(2,1)S(1)}, f32[4,6,576]{2,1,0:T(8,128)}, bf16[4,576,6,64]{1,3,2,0:T(8,128)(2,1)}, s32[4]{0:T(128)...) while((s32[]{:T(128)}, ...), condition=%wide.region_5.6_spmd.clone.clone, body=%wide.region_2.5_spmd.clone.clone.sunk | while | flops 534377664 | bytes 28236528 | solution.py:132
  70.0 3.7 fusion.162
  80.6 3.7 fusion.162
  91.2 3.7 fusion.162
  101.7 3.7 fusion.162
  108.9 3.5 reshape.309
  112.5 6.4 fusion.83
  118.9 16.7 %reduce-scatter.12.cloned.1.call-done = f32[1152,768]{1,0:T(8,128)} async-done(((f32[2304,768]{1,0:T(8,128)}), f32[1152,768]{1,0:T(8,128)}) %reduce-scatter.12.cloned.1.call-update) | async-done | bytes 3538960 | tf_op jit(solution)/shard_map/reduce_scatter | solution.py:134
  143.7 11.9 all-gather.7.cloned.1.call-done
  155.6 10.5 fusion.85
  166.1 6.2 fusion.84
  172.4 14.8 multiply_convert_fusion.1
  187.2 7.5 fusion.86
  194.7 6.1 convolution_add_fusion
  201.0 7.7 convolution_convert_fusion
  208.8 8.7 reduce-scatter.16.cloned.1.call-done
  217.5 3.4 multiply_reduce_fusion.1
  221.5 10.8 reduce-scatter.14.cloned.1.call-done
  232.3 5.9 fusion.80
  238.3 13.9 all-gather.11.cloned.1.call-done
  252.2 4.1 convolution_convert_fusion.1
  258.8 4.3 reshape.310
  264.7 246.6 %while.31 = (s32[]{:T(128)}, f32[4,576,6,64]{1,0,3,2:T(4,128)}, f32[4,576,6,64]{1,0,3,2:T(4,128)}, bf16[4,576,6,64]{1,3,2,0:T(8,128)(2,1)}, bf16[4,576,6,64]{1,3...) while((s32[]{:T(128)}, f32[4,576,6,64]{1,0,3,2:T(4,128)}, ...), condition=%wide.region_13.14_spmd.clone.clone, body=%wide.region_11.13_spmd.clone.clone.sunk | while | flops 1304982784 | bytes 89503072 | solution.py:212
  270.0 3.5 fusion.175
  273.5 4.9 multiply_reduce_fusion.5
  287.4 19.6 %dynamic_update_slice.40 = f32[4,576,6,64]{1,0,3,2:T(4,128)} dynamic-update-slice(f32[4,576,6,64]{1,0,3,2:T(4,128)} %get-tuple-element.483, f32[1,576,6,64]{1,0,3,2:T(1,128)S(1)} %copy.81, s32[]{:T(128)S(6)} %copy.100, s32[]{:T(128)} %constant.88.clone.1..sunk, s32[]{:T(128)} %constant.88.clone.1..sunk, s32[]{:T(128)} %constant.88.clone.1..sunk) | dynamic-update-slice | bytes 1769476 | tf_op jit(solution)/shard_map/while/body/jit(dynamic_update_index_in_dim)/dynamic_update_slice | solution.py:212
  307.0 19.6 %dynamic_update_slice.39 = f32[4,576,6,64]{1,0,3,2:T(4,128)} dynamic-update-slice(f32[4,576,6,64]{1,0,3,2:T(4,128)} %get-tuple-element.482, f32[1,576,6,64]{1,0,3,2:T(1,128)S(1)} %copy.80, s32[]{:T(128)S(6)} %copy.100, s32[]{:T(128)} %constant.88.clone.1..sunk, s32[]{:T(128)} %constant.88.clone.1..sunk, s32[]{:T(128)} %constant.88.clone.1..sunk) | dynamic-update-slice | bytes 1769476 | tf_op jit(solution)/shard_map/while/body/jit(dynamic_update_index_in_dim)/dynamic_update_slice | solution.py:212
  331.5 3.5 fusion.175
  335.0 5.0 multiply_reduce_fusion.5
  348.9 19.6 %dynamic_update_slice.40 = f32[4,576,6,64]{1,0,3,2:T(4,128)} dynamic-update-slice(f32[4,576,6,64]{1,0,3,2:T(4,128)} %get-tuple-element.483, f32[1,576,6,64]{1,0,3,2:T(1,128)S(1)} %copy.81, s32[]{:T(128)S(6)} %copy.100, s32[]{:T(128)} %constant.88.clone.1..sunk, s32[]{:T(128)} %constant.88.clone.1..sunk, s32[]{:T(128)} %constant.88.clone.1..sunk) | dynamic-update-slice | bytes 1769476 | tf_op jit(solution)/shard_map/while/body/jit(dynamic_update_index_in_dim)/dynamic_update_slice | solution.py:212
  368.5 19.6 %dynamic_update_slice.39 = f32[4,576,6,64]{1,0,3,2:T(4,128)} dynamic-update-slice(f32[4,576,6,64]{1,0,3,2:T(4,128)} %get-tuple-element.482, f32[1,576,6,64]{1,0,3,2:T(1,128)S(1)} %copy.80, s32[]{:T(128)S(6)} %copy.100, s32[]{:T(128)} %constant.88.clone.1..sunk, s32[]{:T(128)} %constant.88.clone.1..sunk, s32[]{:T(128)} %constant.88.clone.1..sunk) | dynamic-update-slice | bytes 1769476 | tf_op jit(solution)/shard_map/while/body/jit(dynamic_update_index_in_dim)/dynamic_update_slice | solution.py:212
  393.0 3.5 fusion.175
  396.5 5.0 multiply_reduce_fusion.5
  410.4 19.6 %dynamic_update_slice.40 = f32[4,576,6,64]{1,0,3,2:T(4,128)} dynamic-update-slice(f32[4,576,6,64]{1,0,3,2:T(4,128)} %get-tuple-element.483, f32[1,576,6,64]{1,0,3,2:T(1,128)S(1)} %copy.81, s32[]{:T(128)S(6)} %copy.100, s32[]{:T(128)} %constant.88.clone.1..sunk, s32[]{:T(128)} %constant.88.clone.1..sunk, s32[]{:T(128)} %constant.88.clone.1..sunk) | dynamic-update-slice | bytes 1769476 | tf_op jit(solution)/shard_map/while/body/jit(dynamic_update_index_in_dim)/dynamic_update_slice | solution.py:212
  430.1 19.6 %dynamic_update_slice.39 = f32[4,576,6,64]{1,0,3,2:T(4,128)} dynamic-update-slice(f32[4,576,6,64]{1,0,3,2:T(4,128)} %get-tuple-element.482, f32[1,576,6,64]{1,0,3,2:T(1,128)S(1)} %copy.80, s32[]{:T(128)S(6)} %copy.100, s32[]{:T(128)} %constant.88.clone.1..sunk, s32[]{:T(128)} %constant.88.clone.1..sunk, s32[]{:T(128)} %constant.88.clone.1..sunk) | dynamic-update-slice | bytes 1769476 | tf_op jit(solution)/shard_map/while/body/jit(dynamic_update_index_in_dim)/dynamic_update_slice | solution.py:212
  454.5 3.5 fusion.175
  458.0 5.0 multiply_reduce_fusion.5
  472.0 19.6 %dynamic_update_slice.40 = f32[4,576,6,64]{1,0,3,2:T(4,128)} dynamic-update-slice(f32[4,576,6,64]{1,0,3,2:T(4,128)} %get-tuple-element.483, f32[1,576,6,64]{1,0,3,2:T(1,128)S(1)} %copy.81, s32[]{:T(128)S(6)} %copy.100, s32[]{:T(128)} %constant.88.clone.1..sunk, s32[]{:T(128)} %constant.88.clone.1..sunk, s32[]{:T(128)} %constant.88.clone.1..sunk) | dynamic-update-slice | bytes 1769476 | tf_op jit(solution)/shard_map/while/body/jit(dynamic_update_index_in_dim)/dynamic_update_slice | solution.py:212
  491.6 19.6 %dynamic_update_slice.39 = f32[4,576,6,64]{1,0,3,2:T(4,128)} dynamic-update-slice(f32[4,576,6,64]{1,0,3,2:T(4,128)} %get-tuple-element.482, f32[1,576,6,64]{1,0,3,2:T(1,128)S(1)} %copy.80, s32[]{:T(128)S(6)} %copy.100, s32[]{:T(128)} %constant.88.clone.1..sunk, s32[]{:T(128)} %constant.88.clone.1..sunk, s32[]{:T(128)} %constant.88.clone.1..sunk) | dynamic-update-slice | bytes 1769476 | tf_op jit(solution)/shard_map/while/body/jit(dynamic_update_index_in_dim)/dynamic_update_slice | solution.py:212
  517.1 4.1 reshape.311
  521.2 5.4 reshape.312
  535.0 5.1 add_add_fusion
  540.3 9.0 fusion.95
  549.4 10.8 fusion.93
  560.2 9.1 fusion.94
  569.6 5.1 fusion.92
  574.8 5.6 fusion.91
  580.5 5.1 fusion.89
  585.7 5.8 fusion.90
  591.6 3.4 fusion.67
  595.0 43.0 %all-reduce = (f32[768]{0:T(1024)S(1)}, f32[768]{0:T(1024)S(1)}) all-reduce(f32[768]{0:T(1024)S(1)} %get-tuple-element.261, f32[768]{0:T(1024)S(1)} %copy-done.27), channel_id=1, replica_groups=mesh['dp'=16,'mp'=2] {'dp'}, use_global_device_ids=true, to_apply=%region_17.18 | all-reduce | flops 1536 | bytes 12288 | tf_op jit(solution)/shard_map/psum | solution.py:241
  641.1 5.0 fusion.64
  646.1 48.3 %reduce-scatter.32.cloned.1.call-done = f32[1024,48]{0,1:T(8,128)} async-done(((f32[1024,768]{0,1:T(8,128)}), f32[1024,48]{0,1:T(8,128)}) %reduce-scatter.32.cloned.1.call-update) | async-done | bytes 196624 | tf_op jit(solution)/shard_map/reduce_scatter | solution.py:174
  694.4 135.4 %reduce-scatter.28.cloned.1.call-done = f32[48,1024]{1,0:T(8,128)} async-done(((f32[768,1024]{1,0:T(8,128)}), f32[48,1024]{1,0:T(8,128)}) %reduce-scatter.28.cloned.1.call-update) | async-done | bytes 196624 | tf_op jit(solution)/shard_map/reduce_scatter | solution.py:172
  829.8 135.6 %reduce-scatter.30.cloned.1.call-done = f32[48,1024]{1,0:T(8,128)} async-done(((f32[768,1024]{1,0:T(8,128)}), f32[48,1024]{1,0:T(8,128)}) %reduce-scatter.30.cloned.1.call-update) | async-done | bytes 196624 | tf_op jit(solution)/shard_map/reduce_scatter | solution.py:173
  965.4 128.0 %reduce-scatter.26.cloned.1.call-done = f32[384,48]{0,1:T(8,128)} async-done(((f32[384,768]{0,1:T(8,128)}), f32[384,48]{0,1:T(8,128)}) %reduce-scatter.26.cloned.1.call-update) | async-done | bytes 73744 | tf_op jit(solution)/shard_map/reduce_scatter | solution.py:246
  1093.4 127.9 %reduce-scatter.24.cloned.1.call-done = f32[48,384]{1,0:T(8,128)} async-done(((f32[768,384]{1,0:T(8,128)}), f32[48,384]{1,0:T(8,128)}) %reduce-scatter.24.cloned.1.call-update) | async-done | bytes 73744 | tf_op jit(solution)/shard_map/reduce_scatter | solution.py:245
  1221.2 127.8 %reduce-scatter.20.cloned.1.call-done = f32[48,384]{1,0:T(8,128)} async-done(((f32[768,384]{1,0:T(8,128)}), f32[48,384]{1,0:T(8,128)}) %reduce-scatter.20.cloned.1.call-update) | async-done | bytes 73744 | tf_op jit(solution)/shard_map/reduce_scatter | solution.py:243
  1349.0 127.8 %reduce-scatter.22.cloned.1.call-done = f32[48,384]{1,0:T(8,128)} async-done(((f32[768,384]{1,0:T(8,128)}), f32[48,384]{1,0:T(8,128)}) %reduce-scatter.22.cloned.1.call-update) | async-done | bytes 73744 | tf_op jit(solution)/shard_map/reduce_scatter | solution.py:244
  (219 shorter events, 143.5 us)
Async XLA Ops:
  7.2 165.2 %copy-start = (bf16[1024,768]{1,0:T(8,128)(2,1)S(1)}, bf16[1024,768]{1,0:T(8,128)(2,1)}, u32[]{:S(2)}) copy-start(bf16[1024,768]{1,0:T(8,128)(2,1)} %param.26) | copy-start | bytes 4718596
  7.2 22.0 %all-gather.5.cloned.1.call-start = ((), (), s32[]{:S(2)}) async-start(), calls=%async_computation.11 | async-start | bytes 5308416 | tf_op jit(solution)/shard_map/all_gather | solution.py:85
  9.8 0.6 copy-start.22
  13.6 122.0 %reduce-scatter.12.cloned.1.call-start = ((), (), s32[]{:S(2)}) async-start(), calls=%async_computation.12 | async-start | bytes 10616832 | tf_op jit(solution)/shard_map/reduce_scatter | solution.py:134
  40.0 1.7 copy-start.19
  41.6 3.8 copy-start.17
  41.6 3.8 copy-start.30
  45.5 1.7 copy-start.12
  45.5 1.7 copy-start.13
  55.0 1.7 copy-start.11
  60.4 3.0 copy-start.28
  61.7 2.1 copy-start.14
  112.4 6.4 copy-start.6
  118.9 16.8 %copy-start.4 = (bf16[1152,768]{1,0:T(8,128)(2,1)S(1)}, bf16[1152,768]{1,0:T(8,128)(2,1)}, u32[]{:S(2)}) copy-start(bf16[1152,768]{1,0:T(8,128)(2,1)} %param.16) | copy-start | bytes 5308420
  118.9 21.1 %copy-start.24 = (f32[768]{0:T(1024)S(1)}, f32[768]{0:T(1024)}, u32[]{:S(2)}) copy-start(f32[768]{0:T(1024)} %param.23) | copy-start | bytes 9220
  118.9 36.7 %all-gather.7.cloned.1.call-start = ((), (), s32[]{:S(2)}) async-start(), calls=%async_computation.13 | async-start | bytes 5308416 | tf_op jit(solution)/shard_map/all_gather | solution.py:143
  138.2 1.8 copy-start.2
  140.0 1.9 copy-start.10
  141.6 30.8 %all-gather.9.cloned.1.call-start = ((), (), s32[]{:S(2)}) async-start(), calls=%async_computation.15 | async-start | bytes 5308416 | tf_op jit(solution)/shard_map/all_gather | solution.py:162
  143.4 22.7 %copy-start.32 = (bf16[768,1024]{1,0:T(8,128)(2,1)S(1)}, bf16[768,1024]{1,0:T(8,128)(2,1)}, u32[]{:S(2)}) copy-start(bf16[768,1024]{1,0:T(8,128)(2,1)} %param.24) | copy-start | bytes 4718596
  143.5 74.0 %reduce-scatter.16.cloned.1.call-start = ((), (), s32[]{:S(2)}) async-start(), calls=%async_computation.16 | async-start | bytes 10616832 | tf_op jit(solution)/shard_map/reduce_scatter | solution.py:176
  155.6 10.5 copy-start.31
  187.1 7.5 copy-start.34
  187.1 7.5 copy-start.33
  200.8 31.5 %reduce-scatter.14.cloned.1.call-start = ((), (), s32[]{:S(2)}) async-start(), calls=%async_computation.14 | async-start | bytes 5308416 | tf_op jit(solution)/shard_map/reduce_scatter | solution.py:149
  208.7 8.8 copy-start.3
  208.7 43.5 %all-gather.11.cloned.1.call-start = ((), (), s32[]{:S(2)}) async-start(), calls=%async_computation.17 | async-start | bytes 5308416 | tf_op jit(solution)/shard_map/all_gather | solution.py:184
  238.2 353.4 %reduce-scatter.18.cloned.1.call-start = ((), (), s32[]{:S(2)}) async-start(), calls=%async_computation.18 | async-start | bytes 10616832 | tf_op jit(solution)/shard_map/reduce_scatter | solution.py:229
  258.8 6.0 copy-start.29
  267.3 2.7 copy-start.15
  273.5 5.0 copy-start.16
  328.8 2.7 copy-start.15
  335.0 5.0 copy-start.16
  390.3 2.7 copy-start.15
  396.5 5.0 copy-start.16
  451.8 2.7 copy-start.15
  458.0 5.0 copy-start.16
  529.7 1.1 copy-start.18
  530.0 2.9 copy-start.8
  530.8 2.1 copy-start.20
  532.9 2.1 copy-start.9
  532.9 2.1 copy-start.21
  540.1 154.3 %reduce-scatter.32.cloned.1.call-start = ((), (), s32[]{:S(2)}) async-start(), calls=%async_computation.25 | async-start | bytes 3342336 | tf_op jit(solution)/shard_map/reduce_scatter | solution.py:174
  549.3 280.5 %reduce-scatter.28.cloned.1.call-start = ((), (), s32[]{:S(2)}) async-start(), calls=%async_computation.23 | async-start | bytes 3342336 | tf_op jit(solution)/shard_map/reduce_scatter | solution.py:172
  560.2 9.4 copy-start.7
  560.2 405.2 %reduce-scatter.30.cloned.1.call-start = ((), (), s32[]{:S(2)}) async-start(), calls=%async_computation.24 | async-start | bytes 3342336 | tf_op jit(solution)/shard_map/reduce_scatter | solution.py:173
  569.3 524.1 %reduce-scatter.26.cloned.1.call-start = ((), (), s32[]{:S(2)}) async-start(), calls=%async_computation.22 | async-start | bytes 1253376 | tf_op jit(solution)/shard_map/reduce_scatter | solution.py:246
  574.8 646.5 %reduce-scatter.24.cloned.1.call-start = ((), (), s32[]{:S(2)}) async-start(), calls=%async_computation.21 | async-start | bytes 1253376 | tf_op jit(solution)/shard_map/reduce_scatter | solution.py:245
  580.5 768.6 %reduce-scatter.20.cloned.1.call-start = ((), (), s32[]{:S(2)}) async-start(), calls=%async_computation.19 | async-start | bytes 1253376 | tf_op jit(solution)/shard_map/reduce_scatter | solution.py:243
  585.7 5.9 copy-start.5
  585.7 5.9 copy-start.23
  585.7 5.9 copy-start.25
  585.7 891.1 %reduce-scatter.22.cloned.1.call-start = ((), (), s32[]{:S(2)}) async-start(), calls=%async_computation.20 | async-start | bytes 1253376 | tf_op jit(solution)/shard_map/reduce_scatter | solution.py:244
  591.5 3.5 copy-start.27
  591.5 49.6 %copy-start.26 = (f32[1152]{0:T(1024)S(1)}, f32[1152]{0:T(1024)}, u32[]{:S(2)}) copy-start(f32[1152]{0:T(1024)} %get-tuple-element.327) | copy-start | bytes 13828
  641.1 835.6 %copy-start.1 = (bf16[1024,768]{1,0:T(8,128)(2,1)S(1)}, bf16[1024,768]{1,0:T(8,128)(2,1)}, u32[]{:S(2)}) copy-start(bf16[1024,768]{1,0:T(8,128)(2,1)} %param.26) | copy-start | bytes 4718596
Sparse Core Ops, SparseCore 0:
  13.7 15.3 all-gather.4
  119.0 16.6 reduce-scatter.11
  141.7 13.8 all-gather.6
  157.1 13.8 all-gather.8
  200.9 16.5 reduce-scatter.15
  219.6 12.6 reduce-scatter.13
  238.3 13.8 all-gather.10
  540.2 16.7 reduce-scatter.17
  562.5 131.8 reduce-scatter.31
  699.8 129.9 reduce-scatter.27
  835.4 129.9 reduce-scatter.29
  970.6 122.7 reduce-scatter.25
  1098.7 122.5 reduce-scatter.23
  1226.4 122.5 reduce-scatter.19
  1354.2 122.5 reduce-scatter.21
